TPU v7x, 128 devices: a whole 4x4x4 slice. The times are simulated.
128 devices in a mesh: seq: 4 (over x), tp: 32 (over z, y, core).
Axes of the slice: x: 4, y: 4, z: 4, core: 2. Of those that a mesh axis runs over, the one named last changes fastest.
Arguments:
- hidden_in: bfloat16 [96, 4, 1024], P('tp'), may hold values from -6 to 6
- new_query: bfloat16 [96, 4, 1024], P('tp'), may hold values from -70 to 70
- new_key: bfloat16 [96, 4, 1024], P('tp'), may hold values from -15 to 15
- new_value: bfloat16 [96, 4, 1024], P('tp'), may hold values from -6 to 6
- key_cache: bfloat16 [96, 4096, 1024], P('tp', 'seq'), may hold values from -16 to 16
- value_cache: bfloat16 [96, 4096, 1024], P('tp', 'seq'), may hold values from -6 to 6
- lengths: int32 [96], P('tp'), may hold values from 64 to 4096, as said below
- out_weight: bfloat16 [1024, 1024], replicated, may hold values from -0.1875 to 0.1875
- norm_gain: float32 [1024], replicated, may hold values from 0.5 to 1.5
- router_weight: bfloat16 [1024, 16], replicated, may hold values from -0.1875 to 0.1875
- expert_ids: int32 [96, 4, 2], P('tp'), may hold values from 0 to 15, all different within a row
- gate_weight: bfloat16 [45056, 1024], P(('seq', 'tp')), may hold values from -0.1875 to 0.1875
- up_weight: bfloat16 [45056, 1024], P(('seq', 'tp')), may hold values from -0.1875 to 0.1875
- down_weight: bfloat16 [45056, 1024], P(('seq', 'tp')), may hold values from -0.109375 to 0.109375
Outputs:
- attn_out: bfloat16 [96, 4, 1024], P('tp', None, 'seq')
- layer_out: bfloat16 [96, 4, 1024], P('tp', None, 'seq')
Inputs may be any that keep to these rules, and one draw needn't show every extreme that they name: `lengths`: each length is 4096 or between 64 and 128; some request has 4096.
All inputs are finite; a program needn't handle non-finite values.
Results may differ from a plain program's by a relative error of at most 0.014.
Values may be sent and summed in bfloat16 or wider, within the bound.
A program may use at most 64 MiB of HBM per device.

v0:
```python
import jax
import jax.numpy as jnp
from jax import lax
from jax.sharding import PartitionSpec as P

HEADS = 16
masked_score = -1e30
norm_epsilon = 1e-06


def entering(part, axis, combine, identity):
    place = lax.axis_index(axis)
    gathered = lax.all_gather(part, axis)
    state = jnp.zeros_like(part) + jnp.asarray(identity, part.dtype)

    def one(turn, state):
        return combine(state, lax.dynamic_index_in_dim(gathered, turn, 0, False))

    return lax.fori_loop(0, place, one, state)


def add_counts(former, latter):
    return former + latter


def pick_slot(chosen_ids, earlier):
    onehot = chosen_ids[..., None] == jnp.arange(earlier.shape[2], dtype=jnp.int32)
    return jnp.sum(jnp.where(onehot, earlier[:, :, None, :], 0), axis=3)


def body(
    hidden_in,
    new_query,
    new_key,
    new_value,
    key_cache,
    value_cache,
    lengths,
    out_weight,
    norm_gain,
    router_weight,
    expert_ids,
    gate_weight,
    up_weight,
    down_weight,
):
    req_dev, steps, width = hidden_in.shape
    block = key_cache.shape[1]
    head_size = width // HEADS
    scale = head_size ** (-0.5)
    seq_index = lax.axis_index("seq")
    tp_index = lax.axis_index("tp")
    seq_size = lax.axis_size("seq")
    tp_size = lax.axis_size("tp")
    queries = new_query.reshape(req_dev, steps, HEADS, head_size)
    cache_keys = key_cache.reshape(req_dev, block, HEADS, head_size)
    cache_values = value_cache.reshape(req_dev, block, HEADS, head_size)
    fresh_keys = new_key.reshape(req_dev, steps, HEADS, head_size)
    fresh_values = new_value.reshape(req_dev, steps, HEADS, head_size)
    scores = (
        jnp.einsum("rthe,rphe->rhtp", queries, cache_keys, preferred_element_type=jnp.float32)
        * scale
    )
    positions = seq_index * block + jnp.arange(block, dtype=jnp.int32)
    usable = (positions[None, :] < lengths[:, None])[:, None, None, :]
    scores = jnp.where(usable, scores, masked_score)
    fresh_scores = (
        jnp.einsum("rthe,rshe->rhts", queries, fresh_keys, preferred_element_type=jnp.float32)
        * scale
    )
    causal = (jnp.arange(steps)[:, None] >= jnp.arange(steps)[None, :]) & (seq_index == 0)
    fresh_scores = jnp.where(causal, fresh_scores, masked_score)
    local_max = jnp.maximum(jnp.max(scores, axis=3), jnp.max(fresh_scores, axis=3))
    weights = jnp.where(usable, jnp.exp(scores - local_max[..., None]), 0.0)
    fresh_weights = jnp.where(causal, jnp.exp(fresh_scores - local_max[..., None]), 0.0)
    totals = jnp.sum(weights, axis=3) + jnp.sum(fresh_weights, axis=3)
    gathered_values = jnp.einsum(
        "rhtp,rphe->rhte",
        weights.astype(jnp.bfloat16),
        cache_values,
        preferred_element_type=jnp.float32,
    )
    gathered_values = gathered_values + jnp.einsum(
        "rhts,rshe->rhte",
        fresh_weights.astype(jnp.bfloat16),
        fresh_values,
        preferred_element_type=jnp.float32,
    )
    overall = lax.pmax(local_max, "seq")
    factors = jnp.exp(local_max - overall)
    totals, gathered_values = (
        lax.psum((totals * factors).astype(jnp.bfloat16), "seq").astype(jnp.float32),
        lax.psum((gathered_values * factors[..., None]).astype(jnp.bfloat16), "seq").astype(
            jnp.float32
        ),
    )
    context = (
        (gathered_values / totals[..., None])
        .transpose(0, 2, 1, 3)
        .reshape(req_dev, steps, width)
        .astype(jnp.bfloat16)
    )
    attention = jnp.einsum("rtd,de->rte", context, out_weight, preferred_element_type=jnp.float32)
    feature_block = width // seq_size
    attn_out = lax.dynamic_slice_in_dim(
        attention, seq_index * feature_block, feature_block, 2
    ).astype(jnp.bfloat16)
    residual = hidden_in.astype(jnp.float32) + attention
    normed = (
        residual
        * lax.rsqrt(jnp.mean(residual * residual, axis=-1, keepdims=True) + norm_epsilon)
        * norm_gain
    ).astype(jnp.bfloat16)
    experts = router_weight.shape[1]
    topk = expert_ids.shape[2]
    requests = req_dev * tp_size
    capacity = (5 * requests * topk + 4 * experts - 1) // (4 * experts)
    expert_range = jnp.arange(experts, dtype=jnp.int32)
    local_hits = jnp.sum((expert_ids[..., None] == expert_range).astype(jnp.int32), axis=2)
    counts = jnp.sum(local_hits, axis=0)
    before = entering(counts, "tp", add_counts, jnp.zeros_like(counts))
    earlier = (before[None] + jnp.cumsum(local_hits, axis=0) - local_hits).astype(jnp.int32)
    routing = jnp.concatenate([expert_ids, pick_slot(expert_ids, earlier)], axis=2)
    all_routing = lax.all_gather(routing, "tp", axis=0, tiled=True)
    all_ids = all_routing[:, :, :topk]
    all_slots = all_routing[:, :, topk:]
    all_normed = lax.all_gather(normed, "tp", axis=0, tiled=True)
    logits = jnp.einsum(
        "rtd,de->rte", all_normed, router_weight, preferred_element_type=jnp.float32
    )
    onehot = all_ids[..., None] == expert_range
    chosen = jnp.sum(jnp.where(onehot, logits[:, :, None, :], 0.0), axis=3)
    share = 1.0 / (1.0 + jnp.exp(chosen[:, :, ::-1] - chosen))
    slices = seq_size * tp_size // experts
    mine = (seq_index * tp_size + tp_index) // slices
    match = all_ids == mine
    slot_mine = jnp.sum(jnp.where(match, all_slots, 0), axis=2)
    share_mine = jnp.sum(jnp.where(match, share, 0.0), axis=2)
    kept = jnp.any(match, axis=2) & (slot_mine < capacity)
    select = kept[None] & (slot_mine[None] == jnp.arange(capacity, dtype=jnp.int32)[:, None, None])
    buffer = (
        jnp.einsum(
            "crt,rtd->tcd",
            select.astype(jnp.bfloat16),
            all_normed,
            preferred_element_type=jnp.float32,
        )
        .astype(jnp.bfloat16)
        .reshape(steps * capacity, width)
    )
    contract = (((1,), (1,)), ((), ()))
    gate = lax.dot_general(buffer, gate_weight, contract, preferred_element_type=jnp.float32)
    upward = lax.dot_general(buffer, up_weight, contract, preferred_element_type=jnp.float32)
    inner = (jax.nn.gelu(gate) * upward).astype(jnp.bfloat16)
    produced = jnp.dot(inner, down_weight, preferred_element_type=jnp.float32)
    placed = select.astype(jnp.float32) * share_mine[None]
    term = jnp.einsum(
        "crt,tcd->rtd",
        placed,
        produced.reshape(steps, capacity, width),
        precision=lax.Precision.HIGHEST,
    )
    row_sums = lax.psum_scatter(term.astype(jnp.bfloat16), "tp", scatter_dimension=0, tiled=True)
    mixture = lax.psum_scatter(row_sums, "seq", scatter_dimension=2, tiled=True).astype(jnp.float32)
    own_residual = lax.dynamic_slice_in_dim(residual, seq_index * feature_block, feature_block, 2)
    layer_out = (own_residual + mixture).astype(jnp.bfloat16)
    return (attn_out, layer_out)


def solution(mesh):
    return jax.shard_map(
        body,
        mesh=mesh,
        in_specs=(
            P("tp", None, None),
            P("tp", None, None),
            P("tp", None, None),
            P("tp", None, None),
            P("tp", "seq", None),
            P("tp", "seq", None),
            P("tp"),
            P(),
            P(),
            P(),
            P("tp", None, None),
            P(("seq", "tp"), None),
            P(("seq", "tp"), None),
            P(("seq", "tp"), None),
        ),
        out_specs=(P("tp", None, "seq"), P("tp", None, "seq")),
        check_vma=False,
    )
```

profile of v0, /device:TPU:0, one launch (start us, length us, event | category | flops | bytes accessed | tf_op | source)
XLA Modules:
  0.0 284.9 jit_solution(4095929092177931425)
XLA Ops:
  7.2 1.0 reshape.92
  8.2 8.7 %copy.131 = bf16[3,1024,1024]{1,2,0:T(8,128)(2,1)} copy(bf16[3,1024,1024]{2,1,0:T(8,128)(2,1)} %param.20) | data formatting | bytes 12582912 | tf_op args[4]
  17.6 3.8 %fusion.61 = (f32[3,16,4]{2,1,0:T(8,128)S(1)}, f32[3,16,4,1024]{3,2,1,0:T(4,128)S(1)}) fusion(bf16[3,1024,16,64]{1,3,2,0:T(8,128)(2,1)} %bitcast.35, bf16[3,4,16,64]{3,2,1,0:T(8,128)(2,1)S(1)} %reshape.92, pred[3,1024]{1,0:T(4,128)(4,1)S(1)} %broadcast_compare_fusion), kind=kOutput, calls=%fused_computation.93 | convolution fusion | flops 25755456 | bytes 7106304 | tf_op jit(solution)/shard_map/rthe,rphe->rhtp/dot_general | solution.py:61
  21.5 17.1 %pmax.7 = f32[3,16,4]{2,1,0:T(8,128)S(1)} all-reduce(f32[3,16,4]{2,1,0:T(8,128)S(1)} %max.9), channel_id=1, replica_groups=mesh['seq'=4,'tp'=32] {'seq'}, use_global_device_ids=true, to_apply=%region_2.3 | all-reduce | flops 192 | bytes 1536 | tf_op jit(solution)/shard_map/pmax | solution.py:89
  39.3 8.6 %copy.137 = bf16[3,1024,1024]{1,2,0:T(8,128)(2,1)} copy(bf16[3,1024,1024]{2,1,0:T(8,128)(2,1)} %param.21) | data formatting | bytes 12582912 | tf_op args[5]
  48.0 4.6 %fusion.14 = f32[3,16,4,64]{3,2,1,0:T(4,128)S(1)} fusion(bf16[3,1024,16,64]{1,3,2,0:T(8,128)(2,1)} %bitcast.36, f32[3,16,4,1024]{3,2,1,0:T(4,128)S(1)} %get-tuple-element.49, f32[3,16,4]{2,1,0:T(8,128)S(1)} %max.9, pred[3,1024]{1,0:T(4,128)(4,1)S(1)} %broadcast_compare_fusion), kind=kOutput, calls=%fused_computation.22 | convolution fusion | flops 25755648 | bytes 7130880 | tf_op jit(solution)/shard_map/rhtp,rphe->rhte/dot_general | solution.py:77
  53.1 14.9 %all-reduce.1 = (bf16[3,16,4,64]{3,2,1,0:T(4,128)(2,1)S(1)}, bf16[3,16,4]{2,1,0:T(8,128)(2,1)S(1)}) all-reduce(bf16[3,16,4,64]{3,2,1,0:T(4,128)(2,1)S(1)} %fusion.5, bf16[3,16,4]{2,1,0:T(8,128)(2,1)S(1)} %get-tuple-element.42), channel_id=1, replica_groups=mesh['seq'=4,'tp'=32] {'seq'}, use_global_device_ids=true, to_apply=%region_3.4 | all-reduce | flops 12480 | bytes 49920 | tf_op jit(solution)/shard_map/psum | solution.py:93
  68.9 26.4 %all_gather.15 = bf16[96,4,1024]{2,1,0:T(4,128)(2,1)S(1)} all-gather(bf16[3,4,1024]{2,1,0:T(4,128)(2,1)S(1)} %multiply_convert_fusion), channel_id=1, replica_groups=mesh['seq'=4,'tp'=32] {'tp'}, dimensions={0}, use_global_device_ids=true | all-gather | bytes 811008 | tf_op jit(solution)/shard_map/all_gather | solution.py:127
  95.3 23.6 %all-gather.1 = s32[32,4,16]{2,1,0:T(4,128)S(1)} all-gather(s32[1,4,16]{2,1,0:T(4,128)S(1)} %bitcast.39), channel_id=2, replica_groups=mesh['seq'=4,'tp'=32] {'tp'}, dimensions={0}, use_global_device_ids=true | all-gather | bytes 8448 | tf_op jit(solution)/shard_map/all_gather | solution.py:13
  119.3 23.6 %all_gather.14 = s32[96,4,4]{2,1,0:T(4,128)S(1)} all-gather(s32[3,4,4]{2,1,0:T(4,128)S(1)} %copy.143), channel_id=1, replica_groups=mesh['seq'=4,'tp'=32] {'tp'}, dimensions={0}, use_global_device_ids=true | all-gather | bytes 6336 | tf_op jit(solution)/shard_map/all_gather | solution.py:124
  143.9 0.5 convolution_convert_fusion.1
  144.5 1.5 fusion.62
  145.9 2.0 fusion.7
  148.0 1.4 fusion.2
  149.4 1.5 copy.155
  151.0 0.6 dynamic-slice
  152.2 101.1 %all-reduce.4.cloned.1.call-done = bf16[96,4,1024]{2,1,0:T(4,128)(2,1)} async-done(((bf16[96,4,1024]{2,1,0:T(4,128)(2,1)}), bf16[96,4,1024]{2,1,0:T(4,128)(2,1)}) %all-reduce.4.cloned.1.call-update) | async-done | bytes 786448
  253.3 0.7 constant_dynamic-slice_fusion
  254.1 0.7 copy.156
  254.8 1.2 reshape.105
  256.0 0.6 dynamic-slice_convert_fusion
  256.6 19.6 %reduce-scatter.4.cloned.1.call-done = bf16[256,12]{1,0:T(8,128)(2,1)} async-done(((bf16[1024,12]{1,0:T(8,128)(2,1)}), bf16[256,12]{1,0:T(8,128)(2,1)}) %reduce-scatter.4.cloned.1.call-update) | async-done | bytes 6160
  276.3 1.0 reshape.106
  277.4 0.6 add_convert_fusion
  (66 shorter events, 4.6 us)
Async XLA Ops:
  7.2 61.1 %copy-start = (bf16[1024,1024]{1,0:T(8,128)(2,1)S(1)}, bf16[1024,1024]{1,0:T(8,128)(2,1)}, u32[]{:S(2)}) copy-start(bf16[1024,1024]{1,0:T(8,128)(2,1)} %param.23) | copy-start | bytes 6291460
  7.2 246.2 %all-reduce.4.cloned.1.call-start = ((), (), s32[]{:S(2)}) async-start(), calls=%async_computation.2 | async-start | bytes 1572864
  8.2 8.7 %copy-start.3 = (bf16[3,4,1024]{2,1,0:T(4,128)(2,1)S(1)}, bf16[3,4,1024]{2,1,0:T(4,128)(2,1)}, u32[]{:S(2)}) copy-start(bf16[3,4,1024]{2,1,0:T(4,128)(2,1)} %param.18) | copy-start | bytes 73732
  8.2 9.3 %copy-start.6 = (s32[3]{0:T(128)S(1)}, s32[3]{0:T(128)}, u32[]{:S(2)}) copy-start(s32[3]{0:T(128)} %param.22) | copy-start | bytes 40
  48.0 4.8 %copy-start.4 = (bf16[3,4,1024]{2,1,0:T(4,128)(2,1)S(1)}, bf16[3,4,1024]{2,1,0:T(4,128)(2,1)}, u32[]{:S(2)}) copy-start(bf16[3,4,1024]{2,1,0:T(4,128)(2,1)} %param.19) | copy-start | bytes 73732
  48.0 20.3 %copy-start.2 = (bf16[3,4,1024]{2,1,0:T(4,128)(2,1)S(1)}, bf16[3,4,1024]{2,1,0:T(4,128)(2,1)}, u32[]{:S(2)}) copy-start(bf16[3,4,1024]{2,1,0:T(4,128)(2,1)} %param.16) | copy-start | bytes 73732
  48.0 20.8 %copy-start.5 = (f32[1024]{0:T(1024)S(1)}, f32[1024]{0:T(1024)}, u32[]{:S(2)}) copy-start(f32[1024]{0:T(1024)} %param.24) | copy-start | bytes 12292
  48.0 47.3 %copy-start.1 = (s32[3,4,2]{1,2,0:T(2,128)S(1)}, s32[3,4,2]{1,2,0:T(2,128)}, u32[]{:S(2)}) copy-start(s32[3,4,2]{1,2,0:T(2,128)} %param.26) | copy-start | bytes 292
  48.0 95.2 %copy-start.7 = (bf16[1024,16]{0,1:T(8,128)(2,1)S(1)}, bf16[1024,16]{0,1:T(8,128)(2,1)}, u32[]{:S(2)}) copy-start(bf16[1024,16]{0,1:T(8,128)(2,1)} %param.25) | copy-start | bytes 98308
  68.8 82.2 %copy-start.8 = (u32[128]{0:T(128)S(1)}, u32[128]{0:T(128)}, u32[]{:S(2)}) copy-start(u32[128]{0:T(128)} %constant.85) | copy-start | bytes 1540
  150.9 125.3 %reduce-scatter.4.cloned.1.call-start = ((), (), s32[]{:S(2)}) async-start(), calls=%async_computation.1 | async-start | bytes 327680
Sparse Core Ops, SparseCore 0:
  151.1 102.2 all-reduce.3
  256.1 20.0 reduce-scatter.3
where the time goes:
time: 286 us; the launch traced here: 285 us
  waiting for transfers between devices  121 us (42%)
  blocking collectives  106 us (37%)
  local copies, waits for them, and re-layouts  26.3 us (9%)
  matrix products  15.1 us (5%)
  between operations  15 us (5%)
    unnamed x4, waiting for transfers between devices  121 us
    all_gather x1, blocking collectives, body(): all_normed = lax.all_gather(normed, 'tp', axis=0, tiled=True)  26.4 us
    all_gather x1, blocking collectives, entering(): gathered = lax.all_gather(part, axis)  23.6 us
    all_gather x1, blocking collectives, body(): all_routing = lax.all_gather(routing, 'tp', axis=0, tiled=True)  23.6 us
    unnamed x28, local copies, waits for them, and re-layouts  21.9 us
    pmax x1, blocking collectives, body(): overall = lax.pmax(local_max, 'seq')  17.1 us
    psum x1, blocking collectives, body(): lax.psum((gathered_values * factors[..., None]).astype(jnp.bfloat16), 'seq')  14.9 us
  transfers between devices with their start and end apart: 2, of which 2 were waited for; matrix products, arithmetic and copies ran while one was open for 0% of the time, Pallas kernels for 0%

commit v1 on v0

--- a/solution.py
+++ b/solution.py
@@ -90,9 +90,10 @@
     factors = jnp.exp(local_max - overall)
     totals, gathered_values = (
         lax.psum((totals * factors).astype(jnp.bfloat16), "seq").astype(jnp.float32),
-        lax.psum((gathered_values * factors[..., None]).astype(jnp.bfloat16), "seq").astype(
-            jnp.float32
-        ),
+        jnp.sum(
+            lax.all_gather((gathered_values * factors[..., None]).astype(jnp.bfloat16), "seq"),
+            axis=0,
+        ).astype(jnp.float32),
     )
     context = (
         (gathered_values / totals[..., None])

time: 286 us -> 297 us (1.038)
  blocking collectives: 106 us -> 117 us
    all_gather x0 -> x1, blocking collectives: none -> 12.2 us  [body(): lax.all_gather((gathered_values * factors[..., None]).astype(jnp.bfloat16...]
where the time goes in v1:
time: 297 us; the launch traced here: 296 us
  waiting for transfers between devices  120 us (40%)
  blocking collectives  117 us (39%)
  local copies, waits for them, and re-layouts  26.3 us (9%)
  matrix products  15.1 us (5%)
  between operations  15 us (5%)
    unnamed x4, waiting for transfers between devices  120 us
    all_gather x1, blocking collectives, body(): all_normed = lax.all_gather(normed, 'tp', axis=0, tiled=True)  26.4 us
    all_gather x1, blocking collectives, entering(): gathered = lax.all_gather(part, axis)  23.6 us
    all_gather x1, blocking collectives, body(): all_routing = lax.all_gather(routing, 'tp', axis=0, tiled=True)  23.6 us
    unnamed x28, local copies, waits for them, and re-layouts  21.9 us
    pmax x1, blocking collectives, body(): overall = lax.pmax(local_max, 'seq')  17.1 us
    psum x1, blocking collectives, body(): lax.psum((totals * factors).astype(jnp.bfloat16), 'seq').astype(jnp.float32)  14.3 us
    all_gather x1, blocking collectives, body(): lax.all_gather((gathered_values * factors[..., None]).astype(jnp.bfloat16...  12.2 us
  transfers between devices with their start and end apart: 2, of which 2 were waited for; matrix products, arithmetic and copies ran while one was open for 0% of the time, Pallas kernels for 0%

profile of v1, /device:TPU:0, one launch (start us, length us, event | category | flops | bytes accessed | tf_op | source)
XLA Modules:
  0.0 295.8 jit_solution(14295587785396430981)
XLA Ops:
  7.2 1.0 reshape.92
  8.2 8.7 %copy.161 = bf16[3,1024,1024]{1,2,0:T(8,128)(2,1)} copy(bf16[3,1024,1024]{2,1,0:T(8,128)(2,1)} %param.20) | data formatting | bytes 12582912 | tf_op args[4]
  17.6 3.8 %fusion.62 = (f32[3,16,4]{2,1,0:T(8,128)S(1)}, f32[3,16,4,1024]{3,2,1,0:T(4,128)S(1)}) fusion(bf16[3,1024,16,64]{1,3,2,0:T(8,128)(2,1)} %bitcast.42, bf16[3,4,16,64]{3,2,1,0:T(8,128)(2,1)S(1)} %reshape.92, pred[3,1024]{1,0:T(4,128)(4,1)S(1)} %broadcast_compare_fusion), kind=kOutput, calls=%fused_computation.94 | convolution fusion | flops 25755456 | bytes 7106304 | tf_op jit(solution)/shard_map/rthe,rphe->rhtp/dot_general | solution.py:61
  21.5 17.1 %pmax.7 = f32[3,16,4]{2,1,0:T(8,128)S(1)} all-reduce(f32[3,16,4]{2,1,0:T(8,128)S(1)} %max.9), channel_id=1, replica_groups=mesh['seq'=4,'tp'=32] {'seq'}, use_global_device_ids=true, to_apply=%region_2.3 | all-reduce | flops 192 | bytes 1536 | tf_op jit(solution)/shard_map/pmax | solution.py:89
  39.3 8.6 %copy.167 = bf16[3,1024,1024]{1,2,0:T(8,128)(2,1)} copy(bf16[3,1024,1024]{2,1,0:T(8,128)(2,1)} %param.21) | data formatting | bytes 12582912 | tf_op args[5]
  48.0 4.6 %fusion.14 = f32[3,16,4,64]{3,2,1,0:T(4,128)S(1)} fusion(bf16[3,1024,16,64]{1,3,2,0:T(8,128)(2,1)} %bitcast.43, f32[3,16,4,1024]{3,2,1,0:T(4,128)S(1)} %get-tuple-element.47, f32[3,16,4]{2,1,0:T(8,128)S(1)} %max.9, pred[3,1024]{1,0:T(4,128)(4,1)S(1)} %broadcast_compare_fusion), kind=kOutput, calls=%fused_computation.22 | convolution fusion | flops 25755648 | bytes 7130880 | tf_op jit(solution)/shard_map/rhtp,rphe->rhte/dot_general | solution.py:77
  53.1 12.2 %all-gather = bf16[12,16,4,64]{3,1,2,0:T(8,128)(2,1)S(1)} all-gather(bf16[3,16,4,64]{3,1,2,0:T(8,128)(2,1)S(1)} %copy.171), channel_id=2, replica_groups=mesh['seq'=4,'tp'=32] {'seq'}, dimensions={0}, use_global_device_ids=true | all-gather | bytes 122880 | tf_op jit(solution)/shard_map/all_gather | solution.py:94
  65.5 14.3 %psum.7 = bf16[3,4,16]{1,2,0:T(8,128)(2,1)S(1)} all-reduce(bf16[3,4,16]{1,2,0:T(8,128)(2,1)S(1)} %get-tuple-element.40), channel_id=1, replica_groups=mesh['seq'=4,'tp'=32] {'seq'}, use_global_device_ids=true, to_apply=%region_6.7 | all-reduce | flops 192 | bytes 768 | tf_op jit(solution)/shard_map/psum | solution.py:92
  80.6 26.4 %all_gather.23 = bf16[96,4,1024]{2,1,0:T(4,128)(2,1)S(1)} all-gather(bf16[3,4,1024]{2,1,0:T(4,128)(2,1)S(1)} %multiply_convert_fusion), channel_id=1, replica_groups=mesh['seq'=4,'tp'=32] {'tp'}, dimensions={0}, use_global_device_ids=true | all-gather | bytes 811008 | tf_op jit(solution)/shard_map/all_gather | solution.py:128
  107.1 23.6 %all-gather.2 = s32[32,4,16]{2,1,0:T(4,128)S(1)} all-gather(s32[1,4,16]{2,1,0:T(4,128)S(1)} %bitcast.47), channel_id=3, replica_groups=mesh['seq'=4,'tp'=32] {'tp'}, dimensions={0}, use_global_device_ids=true | all-gather | bytes 8448 | tf_op jit(solution)/shard_map/all_gather | solution.py:13
  131.1 23.6 %all_gather.22 = s32[96,4,4]{2,1,0:T(4,128)S(1)} all-gather(s32[3,4,4]{2,1,0:T(4,128)S(1)} %copy.175), channel_id=1, replica_groups=mesh['seq'=4,'tp'=32] {'tp'}, dimensions={0}, use_global_device_ids=true | all-gather | bytes 6336 | tf_op jit(solution)/shard_map/all_gather | solution.py:125
  156.2 1.5 fusion.63
  157.7 2.0 fusion.7
  159.7 1.4 fusion.2
  161.1 1.5 copy.187
  162.8 0.6 dynamic-slice
  164.0 100.3 %all-reduce.3.cloned.1.call-done = bf16[96,4,1024]{2,1,0:T(4,128)(2,1)} async-done(((bf16[96,4,1024]{2,1,0:T(4,128)(2,1)}), bf16[96,4,1024]{2,1,0:T(4,128)(2,1)}) %all-reduce.3.cloned.1.call-update) | async-done | bytes 786448
  264.3 0.7 constant_dynamic-slice_fusion
  265.0 0.7 copy.188
  265.8 1.2 reshape.106
  267.0 0.6 dynamic-slice_convert_fusion
  267.6 19.6 %reduce-scatter.4.cloned.1.call-done = bf16[256,12]{1,0:T(8,128)(2,1)} async-done(((bf16[1024,12]{1,0:T(8,128)(2,1)}), bf16[256,12]{1,0:T(8,128)(2,1)}) %reduce-scatter.4.cloned.1.call-update) | async-done | bytes 6160
  287.2 1.0 reshape.107
  288.4 0.6 add_convert_fusion
  (70 shorter events, 5.2 us)
Async XLA Ops:
  7.2 72.8 %copy-start = (bf16[1024,1024]{1,0:T(8,128)(2,1)S(1)}, bf16[1024,1024]{1,0:T(8,128)(2,1)}, u32[]{:S(2)}) copy-start(bf16[1024,1024]{1,0:T(8,128)(2,1)} %param.23) | copy-start | bytes 6291460
  7.2 257.1 %all-reduce.3.cloned.1.call-start = ((), (), s32[]{:S(2)}) async-start(), calls=%async_computation.2 | async-start | bytes 1572864
  8.2 8.7 %copy-start.3 = (bf16[3,4,1024]{2,1,0:T(4,128)(2,1)S(1)}, bf16[3,4,1024]{2,1,0:T(4,128)(2,1)}, u32[]{:S(2)}) copy-start(bf16[3,4,1024]{2,1,0:T(4,128)(2,1)} %param.18) | copy-start | bytes 73732
  8.2 9.3 %copy-start.6 = (s32[3]{0:T(128)S(1)}, s32[3]{0:T(128)}, u32[]{:S(2)}) copy-start(s32[3]{0:T(128)} %param.22) | copy-start | bytes 40
  48.0 4.8 %copy-start.4 = (bf16[3,4,1024]{2,1,0:T(4,128)(2,1)S(1)}, bf16[3,4,1024]{2,1,0:T(4,128)(2,1)}, u32[]{:S(2)}) copy-start(bf16[3,4,1024]{2,1,0:T(4,128)(2,1)} %param.19) | copy-start | bytes 73732
  48.0 32.0 %copy-start.2 = (bf16[3,4,1024]{2,1,0:T(4,128)(2,1)S(1)}, bf16[3,4,1024]{2,1,0:T(4,128)(2,1)}, u32[]{:S(2)}) copy-start(bf16[3,4,1024]{2,1,0:T(4,128)(2,1)} %param.16) | copy-start | bytes 73732
  48.0 32.6 %copy-start.5 = (f32[1024]{0:T(1024)S(1)}, f32[1024]{0:T(1024)}, u32[]{:S(2)}) copy-start(f32[1024]{0:T(1024)} %param.24) | copy-start | bytes 12292
  48.0 59.0 %copy-start.1 = (s32[3,4,2]{1,2,0:T(2,128)S(1)}, s32[3,4,2]{1,2,0:T(2,128)}, u32[]{:S(2)}) copy-start(s32[3,4,2]{1,2,0:T(2,128)} %param.26) | copy-start | bytes 292
  48.0 106.9 %copy-start.7 = (bf16[1024,16]{0,1:T(8,128)(2,1)S(1)}, bf16[1024,16]{0,1:T(8,128)(2,1)}, u32[]{:S(2)}) copy-start(bf16[1024,16]{0,1:T(8,128)(2,1)} %param.25) | copy-start | bytes 98308
  80.5 82.2 %copy-start.8 = (u32[128]{0:T(128)S(1)}, u32[128]{0:T(128)}, u32[]{:S(2)}) copy-start(u32[128]{0:T(128)} %constant.87) | copy-start | bytes 1540
  162.7 124.5 %reduce-scatter.4.cloned.1.call-start = ((), (), s32[]{:S(2)}) async-start(), calls=%async_computation.1 | async-start | bytes 327680
Sparse Core Ops, SparseCore 0:
  162.8 101.4 all-reduce.2
  267.1 20.0 reduce-scatter.3
